TPU v7x, 32 devices: a whole 2x2x4 slice. The times are simulated.
32 devices in a mesh: clips: 2 (over y), space: 4 (over z), tm: 2 (over x), chan: 2 (over core).
Axes of the slice: x: 2, y: 2, z: 4, core: 2. Of those that a mesh axis runs over, the one named last changes fastest.
Arguments:
- frames_in: bfloat16 [4, 16, 160, 384], P(('clips', 'tm'), 'space', None, 'chan'), parts along dimension 0, may hold values from -6 to 6
- cache: bfloat16 [4, 16, 160, 384], P('clips', 'space'), parts along dimension 0, may hold values from -6 to 6
- gain_one: bfloat16 [384], replicated, may hold values from 0.099609375 to 1.8984375
- gain_two: bfloat16 [384], replicated, may hold values from 0.099609375 to 1.8984375
- w_query: bfloat16 [384, 384], replicated, may hold values from -10 to 10
- w_key: bfloat16 [384, 384], replicated, may hold values from -10 to 10
- w_value: bfloat16 [384, 384], replicated, may hold values from -0.3125 to 0.3125
- w_out: bfloat16 [384, 384], replicated, may hold values from -0.3125 to 0.3125
- conv_weight: bfloat16 [3, 3, 3, 384, 384], P(None, None, None, None, 'chan'), may hold values from -0.0625 to 0.0625
Outputs:
- decoded: bfloat16 [4, 16, 160, 384], P(('clips', 'tm'), 'space', None, 'chan'), parts along dimension 0
There are 2 independent parts, one for each index of `clips`. A program takes and returns all parts, laid end to end along the dimension named above; an argument that names none is the same for every part. Nothing has to cross between parts.
All inputs are finite; a program needn't handle non-finite values.
Results may differ from a plain program's by a relative error of at most 0.0062.
Values may be sent and summed in bfloat16 or wider, within the bound.
A program may use at most 128 MiB of HBM per device.

v0:
```python
import jax
import jax.numpy as jnp
from jax import lax
from jax.sharding import PartitionSpec as P


def from_behind(array, axis, by):
    devices = lax.axis_size(axis)
    pairs = [(i, i + by) for i in range(devices) if 0 <= i + by < devices]
    return lax.ppermute(array, axis, pairs)


def padded_2(cells, sides, width):
    for axis, dim in sides:
        count = lax.axis_size(axis)
        ends = count - 1
        head = lax.slice_in_dim(cells, 0, width, axis=dim)
        tail = lax.slice_in_dim(cells, cells.shape[dim] - width, cells.shape[dim], axis=dim)
        cells = jnp.concatenate(
            [
                lax.ppermute(tail, axis, [(i, (i + 1) % count) for i in range(ends)]),
                cells,
                lax.ppermute(head, axis, [((i + 1) % count, i) for i in range(ends)]),
            ],
            axis=dim,
        )
    return cells


def rms_scaled(values, gain):
    wide = values.astype(jnp.float32)
    factor = lax.rsqrt(jnp.mean(wide * wide, axis=-1, keepdims=True) + 1e-06)
    return wide * factor * gain.astype(jnp.float32)


def body(frames_in, cache, gain_one, gain_two, w_query, w_key, w_value, w_out, conv_weight):
    mine = lax.axis_index("chan")
    own = lax.all_to_all(frames_in, "chan", split_axis=1, concat_axis=3, tiled=True)
    half_rows, cells, width = (own.shape[1], own.shape[2], own.shape[3])
    tokens = own.reshape(half_rows * cells, width)
    normed = rms_scaled(tokens, gain_one).astype(jnp.bfloat16)
    query = jnp.dot(normed, w_query, preferred_element_type=jnp.float32).astype(jnp.bfloat16)
    scale = width ** (-0.5)
    count = tokens.shape[0]
    piece = lax.all_gather(normed, ("space", "chan"), axis=0, tiled=True)
    keys = jnp.dot(piece, w_key, preferred_element_type=jnp.float32).astype(jnp.bfloat16)
    values = jnp.dot(piece, w_value, preferred_element_type=jnp.float32).astype(jnp.bfloat16)
    top = jnp.full((count, 1), -1e30, jnp.float32)
    scores = jnp.einsum("qc,kc->qk", query, keys, preferred_element_type=jnp.float32) * scale
    new_top = jnp.maximum(top, jnp.max(scores, axis=-1, keepdims=True))
    weights = jnp.exp(scores - new_top)
    total = jnp.sum(weights, axis=-1, keepdims=True)
    accum = jnp.dot(weights.astype(jnp.bfloat16), values, preferred_element_type=jnp.float32)
    top, total, accum = (new_top, total, accum)
    attended = (accum / total).astype(jnp.bfloat16)
    joined = tokens.astype(jnp.float32) + jnp.dot(
        attended, w_out, preferred_element_type=jnp.float32
    )
    joined = joined.astype(jnp.bfloat16).reshape(1, half_rows, cells, width)
    whole = lax.all_gather(joined, "chan", axis=1, tiled=True)
    act = jax.nn.silu(rms_scaled(whole, gain_two)).astype(jnp.bfloat16)
    moment = lax.axis_index("tm")
    first = from_behind(act, "tm", 1)
    second = from_behind(act, "tm", 2)
    prev_one = jnp.where(moment == 0, cache[1:2], first)
    prev_two = jnp.where(moment == 0, cache[0:1], jnp.where(moment == 1, cache[1:2], second))
    stacked = jnp.concatenate([prev_two, prev_one, act], axis=0)
    rimmed = padded_2(stacked, (("space", 1),), 1)
    padded = jnp.pad(rimmed, ((0, 0), (0, 0), (1, 1), (0, 0)))
    conv = lax.conv_general_dilated(
        padded[None],
        conv_weight,
        (1, 1, 1),
        "VALID",
        dimension_numbers=("NDHWC", "DHWIO", "NDHWC"),
        preferred_element_type=jnp.float32,
    )[0]
    share = conv_weight.shape[4]
    own_joined = lax.dynamic_slice_in_dim(whole, mine * share, share, 3)
    return (own_joined.astype(jnp.float32) + conv).astype(jnp.bfloat16)


def solution(mesh):
    return jax.shard_map(
        body,
        mesh=mesh,
        in_specs=(
            P(("clips", "tm"), "space", None, "chan"),
            P("clips", "space", None, None),
            P(),
            P(),
            P(),
            P(),
            P(),
            P(),
            P(None, None, None, None, "chan"),
        ),
        out_specs=P(("clips", "tm"), "space", None, "chan"),
        check_vma=False,
    )
```

profile of v0, /device:TPU:0, one launch (start us, length us, event | category | flops | bytes accessed | tf_op | source)
XLA Modules:
  0.0 116.3 jit_solution(1926624197613109839)
XLA Ops:
  6.5 0.0 copy-start
  6.5 0.0 all-gather.2.cloned.1.call-start
  6.6 5.2 %all_to_all.4 = bf16[1,4,160,192]{3,2,0,1:T(8,128)(2,1)S(1)} all-to-all(bf16[1,4,160,192]{3,2,0,1:T(8,128)(2,1)} %bitcast.55), channel_id=1, replica_groups=mesh['clips'=2,'space'=4,'tm'=2,'chan'=2] {'chan'}, dimensions={1} | all-to-all | bytes 491520 | tf_op jit(solution)/shard_map/all_to_all | solution.py:38
  11.8 0.3 copy.58
  12.1 0.5 reshape.60
  12.6 0.2 multiply_reduce_fusion
  12.9 0.1 rsqrt.20
  13.0 0.0 copy-done.4
  13.0 0.8 multiply_convert_fusion
  13.8 0.0 all-gather.2.cloned.1.call-update
  13.8 0.0 copy-done.5
  13.8 0.0 copy-done.2
  13.8 1.3 %convolution_convert_fusion.2 = bf16[320,384]{1,0:T(8,128)(2,1)S(1)} fusion(bf16[320,384]{1,0:T(8,128)(2,1)} %multiply_convert_fusion, bf16[384,384]{1,0:T(8,128)(2,1)S(1)} %copy-done.2), kind=kOutput, calls=%fused_computation.32 | convolution fusion | flops 94494720 | bytes 786432 | tf_op jit(solution)/shard_map/dot_general | solution.py:42
  15.1 29.6 %all-gather.2.cloned.1.call-done = bf16[2560,384]{1,0:T(8,128)(2,1)} async-done(((bf16[320,384]{1,0:T(8,128)(2,1)}), bf16[2560,384]{1,0:T(8,128)(2,1)}) %all-gather.2.cloned.1.call-update) | async-done | bytes 1966096 | tf_op jit(solution)/shard_map/all_gather | solution.py:45
  44.7 0.0 copy-done
  44.7 5.4 %fusion.46 = (f32[320]{0:T(512)S(1)}, f32[320,2560]{1,0:T(8,128)}) fusion(bf16[320,384]{1,0:T(8,128)(2,1)S(1)} %convolution_convert_fusion.2, bf16[2560,384]{1,0:T(8,128)(2,1)} %all-gather.2.cloned.1.call-done, bf16[384,384]{1,0:T(8,128)(2,1)S(1)} %copy-done), kind=kOutput, calls=%fused_computation.64 | convolution fusion | flops 1386741504 | bytes 5784832 | tf_op jit(solution)/shard_map/qc,kc->qk/dot_general | solution.py:49
  50.1 2.6 %fusion.2 = f32[320]{0:T(512)S(1)} fusion(f32[320,2560]{1,0:T(8,128)} %get-tuple-element.10, f32[320]{0:T(512)S(1)} %broadcast_maximum_fusion), kind=kLoop, calls=%fused_computation.9 | loop fusion | flops 1638080 | bytes 3279360 | tf_op jit(solution)/shard_map/reduce_sum | solution.py:52
  52.7 0.0 copy-done.7
  52.7 0.0 copy-start.3
  52.7 4.8 %fusion.28 = bf16[320,384]{1,0:T(8,128)(2,1)S(1)} fusion(f32[320,2560]{1,0:T(8,128)} %get-tuple-element.10, f32[320]{0:T(512)S(1)} %broadcast_maximum_fusion, bf16[2560,384]{1,0:T(8,128)(2,1)} %all-gather.2.cloned.1.call-done, bf16[384,384]{1,0:T(8,128)(2,1)S(1)} %copy-done.7, f32[320]{0:T(512)S(1)} %fusion.2), kind=kOutput, calls=%fused_computation.35 | convolution fusion | flops 1386987520 | bytes 5786112 | tf_op jit(solution)/shard_map/dot_general | solution.py:53
  57.5 0.0 copy-start.1
  57.5 0.3 fusion.24
  57.9 2.2 %all_gather.7 = bf16[1,4,160,384]{3,2,0,1:T(8,128)(2,1)S(1)} all-gather(bf16[1,2,160,384]{3,2,0,1:T(8,128)(2,1)S(1)} %bitcast.53), channel_id=1, replica_groups=mesh['clips'=2,'space'=4,'tm'=2,'chan'=2] {'chan'}, dimensions={1}, use_global_device_ids=true | all-gather | bytes 737280 | tf_op jit(solution)/shard_map/all_gather | solution.py:60
  60.0 0.2 fusion.31
  60.3 0.4 fusion.38
  60.6 1.4 %collective-permute-start = (bf16[1,4,160,384]{3,2,0,1:T(8,128)(2,1)S(1)}, bf16[1,4,160,384]{3,2,0,1:T(8,128)(2,1)}, u32[]{:S(2)}, u32[]{:S(2)}) collective-permute-start(bf16[1,4,160,384]{3,2,0,1:T(8,128)(2,1)S(1)} %fusion.38), channel_id=1, source_target_pairs={} | collective-permute-start | bytes 1474568 | tf_op jit(solution)/shard_map/ppermute | solution.py:10
  62.1 4.2 %collective-permute-start.1 = (bf16[1,4,160,384]{3,2,0,1:T(8,128)(2,1)S(1)}, bf16[1,4,160,384]{3,2,0,1:T(8,128)(2,1)}, u32[]{:S(2)}, u32[]{:S(2)}) collective-permute-start(bf16[1,4,160,384]{3,2,0,1:T(8,128)(2,1)S(1)} %fusion.38), channel_id=1, source_target_pairs={{0,2},{1,3},{4,6},{5,7},{8,10},{9,11},{12,14},{13,15},{16,18},{17,... | collective-permute-start | bytes 1474568 | tf_op jit(solution)/shard_map/ppermute | solution.py:10
  66.2 0.0 collective-permute-done
  66.2 10.1 %collective-permute-done.1 = bf16[1,4,160,384]{3,2,0,1:T(8,128)(2,1)} collective-permute-done((bf16[1,4,160,384]{3,2,0,1:T(8,128)(2,1)S(1)}, bf16[1,4,160,384]{3,2,0,1:T(8,128)(2,1)}, u32[]{:S(2)}, u32[]{:S(2)}) %collective-permute-start.1) | collective-permute-done | bytes 491552 | tf_op jit(solution)/shard_map/ppermute | solution.py:10
  76.3 1.1 fusion.41
  77.5 1.0 maximum_bitcast_fusion
  78.4 3.5 %collective-permute-start.2 = (bf16[3,1,160,384]{3,2,1,0:T(8,128)(2,1)}, bf16[3,1,160,384]{3,2,1,0:T(8,128)(2,1)S(1)}, u32[]{:S(2)}, u32[]{:S(2)}) collective-permute-start(bf16[3,1,160,384]{3,2,1,0:T(8,128)(2,1)} %get-tuple-element.5), channel_id=1, source_target_pairs={{0,4},{4,8},{8,12},{1,5},{5,9},{9,13},{2,6},{6,10},{10,14},{3,7},{... | collective-permute-start | bytes 1105928 | tf_op jit(solution)/shard_map/ppermute | solution.py:21
  81.9 1.5 %collective-permute-start.3 = (bf16[3,1,160,384]{3,2,1,0:T(8,128)(2,1)}, bf16[3,1,160,384]{3,2,1,0:T(8,128)(2,1)}, u32[]{:S(2)}, u32[]{:S(2)}) collective-permute-start(bf16[3,1,160,384]{3,2,1,0:T(8,128)(2,1)} %get-tuple-element.6), channel_id=1, source_target_pairs={{4,0},{8,4},{12,8},{5,1},{9,5},{13,9},{6,2},{10,6},{14,10},{7,3},{... | collective-permute-start | bytes 1105928 | tf_op jit(solution)/shard_map/ppermute | solution.py:23
  83.4 0.2 constant_dynamic-slice_fusion
  83.6 6.1 %collective-permute-done.2 = bf16[3,1,160,384]{3,2,1,0:T(8,128)(2,1)S(1)} collective-permute-done((bf16[3,1,160,384]{3,2,1,0:T(8,128)(2,1)}, bf16[3,1,160,384]{3,2,1,0:T(8,128)(2,1)S(1)}, u32[]{:S(2)}, u32[]{:S(2)}) %collective-permute-start.2) | collective-permute-done | bytes 368672 | tf_op jit(solution)/shard_map/ppermute | solution.py:21
  89.7 4.1 %collective-permute-done.3 = bf16[3,1,160,384]{3,2,1,0:T(8,128)(2,1)} collective-permute-done((bf16[3,1,160,384]{3,2,1,0:T(8,128)(2,1)}, bf16[3,1,160,384]{3,2,1,0:T(8,128)(2,1)}, u32[]{:S(2)}, u32[]{:S(2)}) %collective-permute-start.3) | collective-permute-done | bytes 368672 | tf_op jit(solution)/shard_map/ppermute | solution.py:23
  93.8 3.1 %fusion.11 = bf16[3,6,1,162,384]{4,3,0,1,2:T(8,128)(2,1)S(1)} fusion(bf16[3,1,160,384]{3,2,0,1:T(8,128)(2,1)} %bitcast.8, bf16[3,1,160,384]{3,2,0,1:T(8,128)(2,1)S(1)} %bitcast.54, bf16[1,4,160,384]{3,2,0,1:T(8,128)(2,1)S(1)} %fusion.38, bf16[1,4,160,384]{3,2,0,1:T(8,128)(2,1)S(1)} %get-tuple-element.8, bf16[1,4,160,384]{3,2,0,1:T(8,128)(2,1)S(1)} %get-tuple-element.7), kind=kLoop, calls=%fused_computation.18 | loop fusion | flops 20155392 | bytes 4451328 | tf_op jit(solution)/shard_map/broadcast_in_dim | solution.py:71
  96.9 1.6 %pad.5 = bf16[3,6,1,168,384]{4,3,0,1,2:T(8,128)(2,1)} pad(bf16[3,6,1,162,384]{4,3,0,1,2:T(8,128)(2,1)S(1)} %fusion.11, bf16[]{:T(256)} %constant.34.clone.1), padding=0_0x0_0x0_0x0_6x0_0 | pad | bytes 4561922 | tf_op jit(solution)/shard_map/broadcast_in_dim | solution.py:71
  98.5 3.5 %reshape.69 = bf16[3,6,1,8,21,384]{5,4,3,0,1,2:T(8,128)(2,1)S(1)} reshape(bf16[3,6,1,168,384]{4,3,0,1,2:T(8,128)(2,1)} %pad.5) | data formatting | bytes 4644864 | tf_op jit(solution)/shard_map/conv_general_dilated | solution.py:70
  102.0 0.0 copy-start.6
  102.0 0.0 copy-start.8
  102.1 0.3 copy.47
  102.4 0.1 slice.19
  102.4 1.7 %copy-done.6 = bf16[3,3,3,384,192]{3,4,2,1,0:T(8,128)(2,1)S(1)} copy-done((bf16[3,3,3,384,192]{3,4,2,1,0:T(8,128)(2,1)S(1)}, bf16[3,3,3,384,192]{3,4,2,1,0:T(8,128)(2,1)}, u32[]{:S(2)}) %copy-start.6) | copy-done | bytes 3981336
  104.2 3.9 %fusion.21 = f32[1,4,8,21,192]{4,2,3,1,0:T(8,128)S(1)} fusion(bf16[3,3,3,384,192]{3,4,2,1,0:T(8,128)(2,1)S(1)} %copy-done.6, bf16[3,6,1,7,2,384]{5,3,4,1,0,2:T(8,128)(2,1)S(1)} %slice.19, bf16[3,6,1,8,21,384]{5,3,4,1,0,2:T(8,128)(2,1)S(1)} %copy.47, pred[8,21]{0,1:T(8,128)(4,1)S(1)} %copy-done.8), kind=kOutput, calls=%fused_computation.28 | convolution fusion | flops 2683201536 | bytes 7013544 | tf_op jit(solution)/shard_map/conv_general_dilated | solution.py:70
  108.1 0.3 copy.48
  108.4 0.3 fusion.40
  108.7 0.8 copy.49
  (14 shorter events, 0.1 us)
Async XLA Ops:
  6.5 38.2 %copy-start = (bf16[384,384]{1,0:T(8,128)(2,1)S(1)}, bf16[384,384]{1,0:T(8,128)(2,1)}, u32[]{:S(2)}) copy-start(bf16[384,384]{1,0:T(8,128)(2,1)} %param.14) | copy-start | bytes 884740
  6.5 6.4 %copy-start.4 = (bf16[384]{0:T(512)(128)(2,1)S(1)}, bf16[384]{0:T(512)(128)(2,1)}, u32[]{:S(2)}) copy-start(bf16[384]{0:T(512)(128)(2,1)} %param.11) | copy-start | bytes 2308
  6.5 7.3 %copy-start.5 = (bf16[384]{0:T(512)(128)(2,1)S(1)}, bf16[384]{0:T(512)(128)(2,1)}, u32[]{:S(2)}) copy-start(bf16[384]{0:T(512)(128)(2,1)} %param.12) | copy-start | bytes 2308
  6.5 7.3 %copy-start.2 = (bf16[384,384]{1,0:T(8,128)(2,1)S(1)}, bf16[384,384]{1,0:T(8,128)(2,1)}, u32[]{:S(2)}) copy-start(bf16[384,384]{1,0:T(8,128)(2,1)} %param.13) | copy-start | bytes 884740
  6.5 38.1 %all-gather.2.cloned.1.call-start = ((), (), s32[]{:S(2)}) async-start(), calls=%async_computation.1 | async-start | bytes 2211840 | tf_op jit(solution)/shard_map/all_gather | solution.py:45
  50.1 2.6 %copy-start.7 = (bf16[384,384]{1,0:T(8,128)(2,1)S(1)}, bf16[384,384]{1,0:T(8,128)(2,1)}, u32[]{:S(2)}) copy-start(bf16[384,384]{1,0:T(8,128)(2,1)} %param.15) | copy-start | bytes 884740
  52.7 4.8 %copy-start.3 = (bf16[384,384]{1,0:T(8,128)(2,1)S(1)}, bf16[384,384]{1,0:T(8,128)(2,1)}, u32[]{:S(2)}) copy-start(bf16[384,384]{1,0:T(8,128)(2,1)} %param.16) | copy-start | bytes 884740
  57.5 18.8 %copy-start.1 = (bf16[2,4,160,384]{3,2,1,0:T(8,128)(2,1)S(1)}, bf16[2,4,160,384]{3,2,1,0:T(8,128)(2,1)}, u32[]{:S(2)}) copy-start(bf16[2,4,160,384]{3,2,1,0:T(8,128)(2,1)} %param.10) | copy-start | bytes 2949124
  60.6 5.6 %collective-permute-start = (bf16[1,4,160,384]{3,2,0,1:T(8,128)(2,1)S(1)}, bf16[1,4,160,384]{3,2,0,1:T(8,128)(2,1)}, u32[]{:S(2)}, u32[]{:S(2)}) collective-permute-start(bf16[1,4,160,384]{3,2,0,1:T(8,128)(2,1)S(1)} %fusion.38), channel_id=1, source_target_pairs={} | collective-permute-start | bytes 1474568 | tf_op jit(solution)/shard_map/ppermute | solution.py:10
  62.1 14.2 %collective-permute-start.1 = (bf16[1,4,160,384]{3,2,0,1:T(8,128)(2,1)S(1)}, bf16[1,4,160,384]{3,2,0,1:T(8,128)(2,1)}, u32[]{:S(2)}, u32[]{:S(2)}) collective-permute-start(bf16[1,4,160,384]{3,2,0,1:T(8,128)(2,1)S(1)} %fusion.38), channel_id=1, source_target_pairs={{0,2},{1,3},{4,6},{5,7},{8,10},{9,11},{12,14},{13,15},{16,18},{17,... | collective-permute-start | bytes 1474568 | tf_op jit(solution)/shard_map/ppermute | solution.py:10
  78.4 11.2 %collective-permute-start.2 = (bf16[3,1,160,384]{3,2,1,0:T(8,128)(2,1)}, bf16[3,1,160,384]{3,2,1,0:T(8,128)(2,1)S(1)}, u32[]{:S(2)}, u32[]{:S(2)}) collective-permute-start(bf16[3,1,160,384]{3,2,1,0:T(8,128)(2,1)} %get-tuple-element.5), channel_id=1, source_target_pairs={{0,4},{4,8},{8,12},{1,5},{5,9},{9,13},{2,6},{6,10},{10,14},{3,7},{... | collective-permute-start | bytes 1105928 | tf_op jit(solution)/shard_map/ppermute | solution.py:21
  81.9 11.9 %collective-permute-start.3 = (bf16[3,1,160,384]{3,2,1,0:T(8,128)(2,1)}, bf16[3,1,160,384]{3,2,1,0:T(8,128)(2,1)}, u32[]{:S(2)}, u32[]{:S(2)}) collective-permute-start(bf16[3,1,160,384]{3,2,1,0:T(8,128)(2,1)} %get-tuple-element.6), channel_id=1, source_target_pairs={{4,0},{8,4},{12,8},{5,1},{9,5},{13,9},{6,2},{10,6},{14,10},{7,3},{... | collective-permute-start | bytes 1105928 | tf_op jit(solution)/shard_map/ppermute | solution.py:23
  102.0 2.1 %copy-start.6 = (bf16[3,3,3,384,192]{3,4,2,1,0:T(8,128)(2,1)S(1)}, bf16[3,3,3,384,192]{3,4,2,1,0:T(8,128)(2,1)}, u32[]{:S(2)}) copy-start(bf16[3,3,3,384,192]{3,4,2,1,0:T(8,128)(2,1)} %param.17) | copy-start | bytes 11943940
  102.0 2.1 %copy-start.8 = (pred[8,21]{0,1:T(8,128)(4,1)S(1)}, pred[8,21]{0,1:T(8,128)(4,1)}, u32[]{:S(2)}) copy-start(pred[8,21]{0,1:T(8,128)(4,1)} %constant.42) | copy-start | bytes 508
Sparse Core Ops, SparseCore 0:
  13.9 30.7 all-gather.1
where the time goes:
time: 117 us; the launch traced here: 116 us
  waiting for transfers between devices  49.9 us (43%)
  matrix products  15.7 us (13%)
  between operations  13.6 us (12%)
  starting transfers between devices  10.6 us (9%)
  other arithmetic  9.76 us (8%)
  local copies, waits for them, and re-layouts  9.41 us (8%)
  blocking collectives  7.34 us (6%)
    all_gather x1, waiting for transfers between devices, body(): piece = lax.all_gather(normed, ('space', 'chan'), axis=0, tiled=True)  29.6 us
    ppermute x2, waiting for transfers between devices, from_behind(): return lax.ppermute(array, axis, pairs)  10.1 us
    ppermute x1, waiting for transfers between devices, padded_2(): lax.ppermute(tail, axis, [(i, (i + 1) % count) for i in range(ends)])  6.08 us
    ppermute x2, starting transfers between devices, from_behind(): return lax.ppermute(array, axis, pairs)  5.6 us
    dot_general x1, matrix products, body(): jnp.einsum('qc,kc->qk', query, keys, preferred_element_type=jnp.float32)  5.41 us
    all_to_all x1, blocking collectives, body(): lax.all_to_all(frames_in, 'chan', split_axis=1, concat_axis=3, tiled=True)  5.19 us
    dot_general x1, matrix products, body(): jnp.dot(weights.astype(jnp.bfloat16), values, preferred_element_type=jnp....  4.79 us
    ppermute x1, waiting for transfers between devices, padded_2(): lax.ppermute(head, axis, [((i + 1) % count, i) for i in range(ends)])  4.14 us
  transfers between devices with their start and end apart: 5, of which 4 were waited for; matrix products, arithmetic and copies ran while one was open for 1% of the time, Pallas kernels for 0%

commit v1 on v0

--- a/solution.py
+++ b/solution.py
@@ -42,7 +42,28 @@
     query = jnp.dot(normed, w_query, preferred_element_type=jnp.float32).astype(jnp.bfloat16)
     scale = width ** (-0.5)
     count = tokens.shape[0]
-    piece = lax.all_gather(normed, ("space", "chan"), axis=0, tiled=True)
+    ways, here, step = (
+        lax.axis_size(("space", "chan")),
+        lax.axis_index(("space", "chan")),
+        normed.shape[0],
+    )
+    shape = [n * ways if d == 0 else n for d, n in enumerate(normed.shape)]
+    piece = lax.dynamic_update_slice_in_dim(
+        jnp.zeros(shape, normed.dtype), normed, here * step, axis=0
+    )
+    going_up = going_down = normed
+    for far in range(1, ways // 2 + 1):
+        going_up = lax.ppermute(
+            going_up, ("space", "chan"), [(d, (d + 1) % ways) for d in range(ways)]
+        )
+        piece = lax.dynamic_update_slice_in_dim(piece, going_up, (here - far) % ways * step, axis=0)
+        if 2 * far < ways:
+            going_down = lax.ppermute(
+                going_down, ("space", "chan"), [(d, (d - 1) % ways) for d in range(ways)]
+            )
+            piece = lax.dynamic_update_slice_in_dim(
+                piece, going_down, (here + far) % ways * step, axis=0
+            )
     keys = jnp.dot(piece, w_key, preferred_element_type=jnp.float32).astype(jnp.bfloat16)
     values = jnp.dot(piece, w_value, preferred_element_type=jnp.float32).astype(jnp.bfloat16)
     top = jnp.full((count, 1), -1e30, jnp.float32)

time: 117 us -> 101 us (0.86)
  starting transfers between devices: 10.6 us -> 24.5 us
  between operations: 13.6 us -> 0.27 us
  waiting for transfers between devices: 49.9 us -> 37.3 us
  blocking collectives: 7.34 us -> 2.16 us
  local copies, waits for them, and re-layouts: 9.41 us -> 12.5 us
  other arithmetic: 9.76 us -> 7.99 us
    all_gather x1 -> x0, waiting for transfers between devices: 29.6 us -> none  [body(): piece = lax.all_gather(normed, ('space', 'chan'), axis=0, tiled=True)]
    ppermute x0 -> x7, waiting for transfers between devices: none -> 16.5 us  [the longest x4 13.2 us: body(): lax.ppermute(going_up, ('space', 'chan'), [(d, (d + 1) % ways) for d in r...]
    ppermute x0 -> x7, starting transfers between devices: none -> 12.2 us  [the longest x3 12 us: body(): lax.ppermute(going_down, ('space', 'chan'), [(d, (d - 1) % ways) for d in...]
    all_to_all x1 -> x0, blocking collectives: 5.19 us -> none  [body(): lax.all_to_all(frames_in, 'chan', split_axis=1, concat_axis=3, tiled=True)]
    all_to_all x0 -> x1, starting transfers between devices: none -> 3.59 us  [body(): lax.all_to_all(frames_in, 'chan', split_axis=1, concat_axis=3, tiled=True)]
    dynamic_update_slice x0 -> x7, local copies, waits for them, and re-layouts: none -> 2.18 us  [the longest x4 1.11 us: body(): lax.dynamic_update_slice_in_dim(piece, going_up, (here - far) % ways * st...]
    ppermute x1, starting transfers between devices: 3.47 us -> 1.3 us  [padded_2(): lax.ppermute(tail, axis, [(i, (i + 1) % count) for i in range(ends)])]
    all_to_all x0 -> x1, waiting for transfers between devices: none -> 1.58 us  [body(): lax.all_to_all(frames_in, 'chan', split_axis=1, concat_axis=3, tiled=True)]
  transfers between devices with their start and end apart: 5 -> 12, of which waited for: 4 -> 9; matrix products, arithmetic and copies ran while one was open for 1% -> 4% of each run, Pallas kernels for 0% -> 0%
where the time goes in v1:
time: 101 us
  waiting for transfers between devices  37.3 us (37%)
  starting transfers between devices  24.5 us (24%)
  matrix products  16 us (16%)
  local copies, waits for them, and re-layouts  12.5 us (12%)
  other arithmetic  7.99 us (8%)
  blocking collectives  2.16 us (2%)
    ppermute x4, waiting for transfers between devices, body(): lax.ppermute(going_up, ('space', 'chan'), [(d, (d + 1) % ways) for d in r...  13.2 us
    ppermute x3, starting transfers between devices, body(): lax.ppermute(going_down, ('space', 'chan'), [(d, (d - 1) % ways) for d in...  12 us
    ppermute x2, waiting for transfers between devices, from_behind(): return lax.ppermute(array, axis, pairs)  9.99 us
    ppermute x2, starting transfers between devices, from_behind(): return lax.ppermute(array, axis, pairs)  5.96 us
    ppermute x1, waiting for transfers between devices, padded_2(): lax.ppermute(tail, axis, [(i, (i + 1) % count) for i in range(ends)])  5.5 us
    dot_general x1, matrix products, body(): jnp.dot(weights.astype(jnp.bfloat16), values, preferred_element_type=jnp....  4.88 us
    dot_general x1, matrix products, body(): jnp.einsum('qc,kc->qk', query, keys, preferred_element_type=jnp.float32)  4.85 us
    conv_general_dilated x4, local copies, waits for them, and re-layouts, body(): lax.conv_general_dilated(padded[None], conv_weight, (1, 1, 1), 'VALID', d...  4.14 us
  transfers between devices with their start and end apart: 12, of which 9 were waited for; matrix products, arithmetic and copies ran while one was open for 4% of the time, Pallas kernels for 0%

profile of v1, /device:TPU:0, one launch (start us, length us, event | category | flops | bytes accessed | tf_op | source)
XLA Modules:
  0.0 100.8 jit_solution(11818649885662151159)
XLA Ops:
  0.0 3.6 %all-to-all-start = ((bf16[1,4,160,192]{3,2,0,1:T(8,128)(2,1)}), bf16[1,4,160,192]{3,2,0,1:T(8,128)(2,1)S(1)}, u32[]{:S(2)}, u32[]{:S(2)}) async-start(bf16[1,4,160,192]{3,2,0,1:T(8,128)(2,1)} %bitcast.56), calls=%async_computation | async-start | bytes 655360 | tf_op jit(solution)/shard_map/all_to_all | solution.py:38
  3.6 1.6 %all-to-all-done = bf16[1,4,160,192]{3,2,0,1:T(8,128)(2,1)S(1)} async-done(((bf16[1,4,160,192]{3,2,0,1:T(8,128)(2,1)}), bf16[1,4,160,192]{3,2,0,1:T(8,128)(2,1)S(1)}, u32[]{:S(2)}, u32[]{:S(2)}) %all-to-all-start) | async-done | bytes 245792 | tf_op jit(solution)/shard_map/all_to_all | solution.py:38
  5.2 0.3 copy.58
  5.5 0.5 reshape.60
  6.1 0.2 multiply_reduce_fusion
  6.3 0.1 rsqrt.20
  6.4 0.2 broadcast_in_dim.6
  6.6 0.2 constant_dynamic-update-slice_fusion.7
  6.8 0.2 collective-permute-start
  7.0 4.7 %collective-permute-start.1 = (bf16[320,384]{1,0:T(8,128)(2,1)S(1)}, bf16[320,384]{1,0:T(8,128)(2,1)}, u32[]{:S(2)}, u32[]{:S(2)}) collective-permute-start(bf16[320,384]{1,0:T(8,128)(2,1)S(1)} %get-tuple-element.6), channel_id=1, source_target_pairs={{0,13},{1,0},{4,1},{5,4},{8,5},{9,8},{12,9},{13,12},{2,15},{3,2},{... | collective-permute-start | bytes 737288 | tf_op jit(solution)/shard_map/ppermute | solution.py:61
  11.7 4.2 %collective-permute-done = bf16[320,384]{1,0:T(8,128)(2,1)} collective-permute-done((bf16[320,384]{1,0:T(8,128)(2,1)S(1)}, bf16[320,384]{1,0:T(8,128)(2,1)}, u32[]{:S(2)}, u32[]{:S(2)}) %collective-permute-start) | collective-permute-done | bytes 245792 | tf_op jit(solution)/shard_map/ppermute | solution.py:56
  15.9 3.7 %collective-permute-start.3 = (bf16[320,384]{1,0:T(8,128)(2,1)}, bf16[320,384]{1,0:T(8,128)(2,1)S(1)}, u32[]{:S(2)}, u32[]{:S(2)}) collective-permute-start(bf16[320,384]{1,0:T(8,128)(2,1)} %collective-permute-done.1), channel_id=1, source_target_pairs={{0,13},{1,0},{4,1},{5,4},{8,5},{9,8},{12,9},{13,12},{2,15},{3,2},{... | collective-permute-start | bytes 737288 | tf_op jit(solution)/shard_map/ppermute | solution.py:61
  19.6 1.0 %convolution_convert_fusion.2 = bf16[320,384]{1,0:T(8,128)(2,1)} fusion(bf16[320,384]{1,0:T(8,128)(2,1)S(1)} %get-tuple-element.6, bf16[384,384]{1,0:T(8,128)(2,1)S(1)} %copy-done.3), kind=kOutput, calls=%fused_computation.32 | convolution fusion | flops 94494720 | bytes 786432 | tf_op jit(solution)/shard_map/dot_general | solution.py:42
  20.6 3.0 %collective-permute-done.2 = bf16[320,384]{1,0:T(8,128)(2,1)S(1)} collective-permute-done((bf16[320,384]{1,0:T(8,128)(2,1)}, bf16[320,384]{1,0:T(8,128)(2,1)S(1)}, u32[]{:S(2)}, u32[]{:S(2)}) %collective-permute-start.2) | collective-permute-done | bytes 245792 | tf_op jit(solution)/shard_map/ppermute | solution.py:56
  23.7 1.0 constant_dynamic-update-slice_fusion.6
  24.6 1.0 constant_dynamic-update-slice_fusion.5
  25.6 3.6 %collective-permute-start.5 = (bf16[320,384]{1,0:T(8,128)(2,1)S(1)}, bf16[320,384]{1,0:T(8,128)(2,1)S(1)}, u32[]{:S(2)}, u32[]{:S(2)}) collective-permute-start(bf16[320,384]{1,0:T(8,128)(2,1)S(1)} %collective-permute-done.3), channel_id=1, source_target_pairs={{0,13},{1,0},{4,1},{5,4},{8,5},{9,8},{12,9},{13,12},{2,15},{3,2},{... | collective-permute-start | bytes 737288 | tf_op jit(solution)/shard_map/ppermute | solution.py:61
  29.3 1.9 %collective-permute-done.4 = bf16[320,384]{1,0:T(8,128)(2,1)S(1)} collective-permute-done((bf16[320,384]{1,0:T(8,128)(2,1)S(1)}, bf16[320,384]{1,0:T(8,128)(2,1)S(1)}, u32[]{:S(2)}, u32[]{:S(2)}) %collective-permute-start.4) | collective-permute-done | bytes 245792 | tf_op jit(solution)/shard_map/ppermute | solution.py:56
  31.3 3.2 %collective-permute-done.5 = bf16[320,384]{1,0:T(8,128)(2,1)S(1)} collective-permute-done((bf16[320,384]{1,0:T(8,128)(2,1)S(1)}, bf16[320,384]{1,0:T(8,128)(2,1)S(1)}, u32[]{:S(2)}, u32[]{:S(2)}) %collective-permute-start.5) | collective-permute-done | bytes 245792 | tf_op jit(solution)/shard_map/ppermute | solution.py:61
  34.5 4.1 %collective-permute-done.6 = bf16[320,384]{1,0:T(8,128)(2,1)S(1)} collective-permute-done((bf16[320,384]{1,0:T(8,128)(2,1)S(1)}, bf16[320,384]{1,0:T(8,128)(2,1)S(1)}, u32[]{:S(2)}, u32[]{:S(2)}) %collective-permute-start.6) | collective-permute-done | bytes 245792 | tf_op jit(solution)/shard_map/ppermute | solution.py:56
  38.7 4.9 %fusion.46 = (f32[320]{0:T(512)S(1)}, f32[320,2560]{1,0:T(8,128)}) fusion(bf16[320,384]{1,0:T(8,128)(2,1)} %convolution_convert_fusion.2, bf16[2560,384]{1,0:T(8,128)(2,1)S(1)} %constant_dynamic-update-slice_fusion, bf16[384,384]{1,0:T(8,128)(2,1)S(1)} %copy-done), kind=kOutput, calls=%fused_computation.72 | convolution fusion | flops 1386741504 | bytes 5784832 | tf_op jit(solution)/shard_map/qc,kc->qk/dot_general | solution.py:70
  43.6 2.6 %fusion.2 = f32[320]{0:T(512)S(1)} fusion(f32[320,2560]{1,0:T(8,128)} %get-tuple-element.12, f32[320]{0:T(512)S(1)} %broadcast_maximum_fusion), kind=kLoop, calls=%fused_computation.9 | loop fusion | flops 1638080 | bytes 3279360 | tf_op jit(solution)/shard_map/reduce_sum | solution.py:73
  46.1 4.9 %fusion.28 = bf16[320,384]{1,0:T(8,128)(2,1)} fusion(bf16[2560,384]{1,0:T(8,128)(2,1)S(1)} %constant_dynamic-update-slice_fusion, bf16[384,384]{1,0:T(8,128)(2,1)S(1)} %copy-done.8, f32[320,2560]{1,0:T(8,128)} %get-tuple-element.12, f32[320]{0:T(512)S(1)} %broadcast_maximum_fusion, f32[320]{0:T(512)S(1)} %fusion.2), kind=kOutput, calls=%fused_computation.35 | convolution fusion | flops 1386987520 | bytes 5786112 | tf_op jit(solution)/shard_map/dot_general | solution.py:74
  51.0 1.4 %fusion.24 = bf16[320,384]{1,0:T(8,128)(2,1)S(1)} fusion(f32[320,384]{1,0:T(8,128)S(1)} %reshape.60, bf16[320,384]{1,0:T(8,128)(2,1)} %fusion.28, bf16[384,384]{1,0:T(8,128)(2,1)S(1)} %copy-done.4), kind=kOutput, calls=%fused_computation.33 | convolution fusion | flops 94617600 | bytes 1277952 | tf_op jit(solution)/shard_map/dot_general | solution.py:77
  52.4 2.2 %all_gather.3 = bf16[1,4,160,384]{3,2,0,1:T(8,128)(2,1)S(1)} all-gather(bf16[1,2,160,384]{3,2,0,1:T(8,128)(2,1)S(1)} %bitcast.53), channel_id=1, replica_groups=mesh['clips'=2,'space'=4,'tm'=2,'chan'=2] {'chan'}, dimensions={1}, use_global_device_ids=true | all-gather | bytes 737280 | tf_op jit(solution)/shard_map/all_gather | solution.py:81
  54.6 0.2 fusion.31
  54.8 0.4 fusion.38
  55.2 1.4 %collective-permute-start.7 = (bf16[1,4,160,384]{3,2,0,1:T(8,128)(2,1)S(1)}, bf16[1,4,160,384]{3,2,0,1:T(8,128)(2,1)}, u32[]{:S(2)}, u32[]{:S(2)}) collective-permute-start(bf16[1,4,160,384]{3,2,0,1:T(8,128)(2,1)S(1)} %fusion.38), channel_id=1, source_target_pairs={} | collective-permute-start | bytes 1474568 | tf_op jit(solution)/shard_map/ppermute | solution.py:10
  56.6 4.5 %collective-permute-start.8 = (bf16[1,4,160,384]{3,2,0,1:T(8,128)(2,1)S(1)}, bf16[1,4,160,384]{3,2,0,1:T(8,128)(2,1)}, u32[]{:S(2)}, u32[]{:S(2)}) collective-permute-start(bf16[1,4,160,384]{3,2,0,1:T(8,128)(2,1)S(1)} %fusion.38), channel_id=1, source_target_pairs={{0,2},{1,3},{4,6},{5,7},{8,10},{9,11},{12,14},{13,15},{16,18},{17,... | collective-permute-start | bytes 1474568 | tf_op jit(solution)/shard_map/ppermute | solution.py:10
  61.1 10.0 %collective-permute-done.8 = bf16[1,4,160,384]{3,2,0,1:T(8,128)(2,1)} collective-permute-done((bf16[1,4,160,384]{3,2,0,1:T(8,128)(2,1)S(1)}, bf16[1,4,160,384]{3,2,0,1:T(8,128)(2,1)}, u32[]{:S(2)}, u32[]{:S(2)}) %collective-permute-start.8) | collective-permute-done | bytes 491552 | tf_op jit(solution)/shard_map/ppermute | solution.py:10
  71.1 1.1 %fusion.41 = (bf16[1,4,160,384]{3,2,0,1:T(8,128)(2,1)S(1)}, bf16[1,4,160,384]{3,2,0,1:T(8,128)(2,1)S(1)}) fusion(bf16[1,4,160,384]{3,2,0,1:T(8,128)(2,1)} %collective-permute-done.7, bf16[2,4,160,384]{3,2,1,0:T(8,128)(2,1)S(1)} %copy-done.2, pred[]{:T(512)S(6)} %eq.16, pred[]{:T(512)S(6)} %eq.15, bf16[1,4,160,384]{3,2,0,1:T(8,128)(2,1)} %collective-permute-done.8), kind=kLoop, calls=%fused_computation.51 | loop fusion | flops 737280 | bytes 2949122 | tf_op jit(solution)/shard_map/jit(_where)/select_n | solution.py:87
  72.3 0.8 maximum_bitcast_fusion
  73.1 1.3 %collective-permute-start.9 = (bf16[3,1,160,384]{3,2,1,0:T(8,128)(2,1)}, bf16[3,1,160,384]{3,2,1,0:T(8,128)(2,1)S(1)}, u32[]{:S(2)}, u32[]{:S(2)}) collective-permute-start(bf16[3,1,160,384]{3,2,1,0:T(8,128)(2,1)} %get-tuple-element.7), channel_id=1, source_target_pairs={{0,4},{4,8},{8,12},{1,5},{5,9},{9,13},{2,6},{6,10},{10,14},{3,7},{... | collective-permute-start | bytes 1105928 | tf_op jit(solution)/shard_map/ppermute | solution.py:21
  74.4 1.5 %collective-permute-start.10 = (bf16[3,1,160,384]{3,2,1,0:T(8,128)(2,1)S(1)}, bf16[3,1,160,384]{3,2,1,0:T(8,128)(2,1)S(1)}, u32[]{:S(2)}, u32[]{:S(2)}) collective-permute-start(bf16[3,1,160,384]{3,2,1,0:T(8,128)(2,1)S(1)} %get-tuple-element.8), channel_id=1, source_target_pairs={{4,0},{8,4},{12,8},{5,1},{9,5},{13,9},{6,2},{10,6},{14,10},{7,3},{... | collective-permute-start | bytes 1105928 | tf_op jit(solution)/shard_map/ppermute | solution.py:23
  75.9 0.9 constant_dynamic-slice_fusion
  76.8 5.5 %collective-permute-done.9 = bf16[3,1,160,384]{3,2,1,0:T(8,128)(2,1)S(1)} collective-permute-done((bf16[3,1,160,384]{3,2,1,0:T(8,128)(2,1)}, bf16[3,1,160,384]{3,2,1,0:T(8,128)(2,1)S(1)}, u32[]{:S(2)}, u32[]{:S(2)}) %collective-permute-start.9) | collective-permute-done | bytes 368672 | tf_op jit(solution)/shard_map/ppermute | solution.py:21
  82.3 3.8 %collective-permute-done.10 = bf16[3,1,160,384]{3,2,1,0:T(8,128)(2,1)S(1)} collective-permute-done((bf16[3,1,160,384]{3,2,1,0:T(8,128)(2,1)S(1)}, bf16[3,1,160,384]{3,2,1,0:T(8,128)(2,1)S(1)}, u32[]{:S(2)}, u32[]{:S(2)}) %collective-permute-start.10) | collective-permute-done | bytes 368672 | tf_op jit(solution)/shard_map/ppermute | solution.py:23
  86.1 2.1 %fusion.11 = bf16[3,6,1,162,384]{4,3,0,1,2:T(8,128)(2,1)S(1)} fusion(bf16[3,1,160,384]{3,2,0,1:T(8,128)(2,1)S(1)} %bitcast.55, bf16[3,1,160,384]{3,2,0,1:T(8,128)(2,1)S(1)} %bitcast.54, bf16[1,4,160,384]{3,2,0,1:T(8,128)(2,1)S(1)} %fusion.38, bf16[1,4,160,384]{3,2,0,1:T(8,128)(2,1)S(1)} %get-tuple-element.10, bf16[1,4,160,384]{3,2,0,1:T(8,128)(2,1)S(1)} %get-tuple-element.9), kind=kLoop, calls=%fused_computation.18 | loop fusion | flops 20155392 | bytes 4451328 | tf_op jit(solution)/shard_map/broadcast_in_dim | solution.py:92
  88.2 1.6 %pad.5 = bf16[3,6,1,168,384]{4,3,0,1,2:T(8,128)(2,1)} pad(bf16[3,6,1,162,384]{4,3,0,1,2:T(8,128)(2,1)S(1)} %fusion.11, bf16[]{:T(256)} %constant.72.clone.1), padding=0_0x0_0x0_0x0_6x0_0 | pad | bytes 4561922 | tf_op jit(solution)/shard_map/broadcast_in_dim | solution.py:92
  89.9 3.5 %reshape.69 = bf16[3,6,1,8,21,384]{5,4,3,0,1,2:T(8,128)(2,1)S(1)} reshape(bf16[3,6,1,168,384]{4,3,0,1,2:T(8,128)(2,1)} %pad.5) | data formatting | bytes 4644864 | tf_op jit(solution)/shard_map/conv_general_dilated | solution.py:91
  93.4 0.0 copy-start.9
  93.4 0.3 copy.47
  93.7 0.1 slice.19
  93.8 1.7 %copy-done.7 = bf16[3,3,3,384,192]{3,4,2,1,0:T(8,128)(2,1)S(1)} copy-done((bf16[3,3,3,384,192]{3,4,2,1,0:T(8,128)(2,1)S(1)}, bf16[3,3,3,384,192]{3,4,2,1,0:T(8,128)(2,1)}, u32[]{:S(2)}) %copy-start.7) | copy-done | bytes 3981336
  95.5 3.9 %fusion.21 = f32[1,4,8,21,192]{4,2,3,1,0:T(8,128)S(1)} fusion(bf16[3,3,3,384,192]{3,4,2,1,0:T(8,128)(2,1)S(1)} %copy-done.7, bf16[3,6,1,7,2,384]{5,3,4,1,0,2:T(8,128)(2,1)S(1)} %slice.19, bf16[3,6,1,8,21,384]{5,3,4,1,0,2:T(8,128)(2,1)S(1)} %copy.47, pred[8,21]{0,1:T(8,128)(4,1)S(1)} %copy-done.9), kind=kOutput, calls=%fused_computation.28 | convolution fusion | flops 2683201536 | bytes 7013544 | tf_op jit(solution)/shard_map/conv_general_dilated | solution.py:91
  99.4 0.3 copy.48
  99.7 0.3 fusion.40
  100.1 0.8 copy.49
  (36 shorter events, 0.3 us)
Async XLA Ops:
  0.0 38.7 %copy-start = (bf16[384,384]{1,0:T(8,128)(2,1)S(1)}, bf16[384,384]{1,0:T(8,128)(2,1)}, u32[]{:S(2)}) copy-start(bf16[384,384]{1,0:T(8,128)(2,1)} %param.14) | copy-start | bytes 884740
  0.0 6.4 %copy-start.5 = (bf16[384]{0:T(512)(128)(2,1)S(1)}, bf16[384]{0:T(512)(128)(2,1)}, u32[]{:S(2)}) copy-start(bf16[384]{0:T(512)(128)(2,1)} %param.11) | copy-start | bytes 2308
  0.0 5.2 %all-to-all-start = ((bf16[1,4,160,192]{3,2,0,1:T(8,128)(2,1)}), bf16[1,4,160,192]{3,2,0,1:T(8,128)(2,1)S(1)}, u32[]{:S(2)}, u32[]{:S(2)}) async-start(bf16[1,4,160,192]{3,2,0,1:T(8,128)(2,1)} %bitcast.56), calls=%async_computation | async-start | bytes 655360 | tf_op jit(solution)/shard_map/all_to_all | solution.py:38
  5.5 14.1 %copy-start.3 = (bf16[384,384]{1,0:T(8,128)(2,1)S(1)}, bf16[384,384]{1,0:T(8,128)(2,1)}, u32[]{:S(2)}) copy-start(bf16[384,384]{1,0:T(8,128)(2,1)} %param.13) | copy-start | bytes 884740
  6.0 14.6 %copy-start.6 = (bf16[384]{0:T(512)(128)(2,1)S(1)}, bf16[384]{0:T(512)(128)(2,1)}, u32[]{:S(2)}) copy-start(bf16[384]{0:T(512)(128)(2,1)} %param.12) | copy-start | bytes 2308
  6.8 9.1 %collective-permute-start = (bf16[320,384]{1,0:T(8,128)(2,1)S(1)}, bf16[320,384]{1,0:T(8,128)(2,1)}, u32[]{:S(2)}, u32[]{:S(2)}) collective-permute-start(bf16[320,384]{1,0:T(8,128)(2,1)S(1)} %get-tuple-element.6), channel_id=1, source_target_pairs={{0,1},{1,4},{4,5},{5,8},{8,9},{9,12},{12,13},{13,0},{2,3},{3,6},{6... | collective-permute-start | bytes 737288 | tf_op jit(solution)/shard_map/ppermute | solution.py:56
  7.0 8.9 %collective-permute-start.1 = (bf16[320,384]{1,0:T(8,128)(2,1)S(1)}, bf16[320,384]{1,0:T(8,128)(2,1)}, u32[]{:S(2)}, u32[]{:S(2)}) collective-permute-start(bf16[320,384]{1,0:T(8,128)(2,1)S(1)} %get-tuple-element.6), channel_id=1, source_target_pairs={{0,13},{1,0},{4,1},{5,4},{8,5},{9,8},{12,9},{13,12},{2,15},{3,2},{... | collective-permute-start | bytes 737288 | tf_op jit(solution)/shard_map/ppermute | solution.py:61
  15.9 7.8 %collective-permute-start.2 = (bf16[320,384]{1,0:T(8,128)(2,1)}, bf16[320,384]{1,0:T(8,128)(2,1)S(1)}, u32[]{:S(2)}, u32[]{:S(2)}) collective-permute-start(bf16[320,384]{1,0:T(8,128)(2,1)} %collective-permute-done), channel_id=1, source_target_pairs={{0,1},{1,4},{4,5},{5,8},{8,9},{9,12},{12,13},{13,0},{2,3},{3,6},{6... | collective-permute-start | bytes 737288 | tf_op jit(solution)/shard_map/ppermute | solution.py:56
  15.9 9.8 %collective-permute-start.3 = (bf16[320,384]{1,0:T(8,128)(2,1)}, bf16[320,384]{1,0:T(8,128)(2,1)S(1)}, u32[]{:S(2)}, u32[]{:S(2)}) collective-permute-start(bf16[320,384]{1,0:T(8,128)(2,1)} %collective-permute-done.1), channel_id=1, source_target_pairs={{0,13},{1,0},{4,1},{5,4},{8,5},{9,8},{12,9},{13,12},{2,15},{3,2},{... | collective-permute-start | bytes 737288 | tf_op jit(solution)/shard_map/ppermute | solution.py:61
  23.6 7.5 %collective-permute-start.4 = (bf16[320,384]{1,0:T(8,128)(2,1)S(1)}, bf16[320,384]{1,0:T(8,128)(2,1)S(1)}, u32[]{:S(2)}, u32[]{:S(2)}) collective-permute-start(bf16[320,384]{1,0:T(8,128)(2,1)S(1)} %collective-permute-done.2), channel_id=1, source_target_pairs={{0,1},{1,4},{4,5},{5,8},{8,9},{9,12},{12,13},{13,0},{2,3},{3,6},{6... | collective-permute-start | bytes 737288 | tf_op jit(solution)/shard_map/ppermute | solution.py:56
  25.6 8.8 %collective-permute-start.5 = (bf16[320,384]{1,0:T(8,128)(2,1)S(1)}, bf16[320,384]{1,0:T(8,128)(2,1)S(1)}, u32[]{:S(2)}, u32[]{:S(2)}) collective-permute-start(bf16[320,384]{1,0:T(8,128)(2,1)S(1)} %collective-permute-done.3), channel_id=1, source_target_pairs={{0,13},{1,0},{4,1},{5,4},{8,5},{9,8},{12,9},{13,12},{2,15},{3,2},{... | collective-permute-start | bytes 737288 | tf_op jit(solution)/shard_map/ppermute | solution.py:61
  31.2 7.5 %collective-permute-start.6 = (bf16[320,384]{1,0:T(8,128)(2,1)S(1)}, bf16[320,384]{1,0:T(8,128)(2,1)S(1)}, u32[]{:S(2)}, u32[]{:S(2)}) collective-permute-start(bf16[320,384]{1,0:T(8,128)(2,1)S(1)} %collective-permute-done.4), channel_id=1, source_target_pairs={{0,1},{1,4},{4,5},{5,8},{8,9},{9,12},{12,13},{13,0},{2,3},{3,6},{6... | collective-permute-start | bytes 737288 | tf_op jit(solution)/shard_map/ppermute | solution.py:56
  43.6 2.6 %copy-start.8 = (bf16[384,384]{1,0:T(8,128)(2,1)S(1)}, bf16[384,384]{1,0:T(8,128)(2,1)}, u32[]{:S(2)}) copy-start(bf16[384,384]{1,0:T(8,128)(2,1)} %param.15) | copy-start | bytes 884740
  46.1 4.9 %copy-start.4 = (bf16[384,384]{1,0:T(8,128)(2,1)S(1)}, bf16[384,384]{1,0:T(8,128)(2,1)}, u32[]{:S(2)}) copy-start(bf16[384,384]{1,0:T(8,128)(2,1)} %param.16) | copy-start | bytes 884740
  51.0 20.1 %copy-start.2 = (bf16[2,4,160,384]{3,2,1,0:T(8,128)(2,1)S(1)}, bf16[2,4,160,384]{3,2,1,0:T(8,128)(2,1)}, u32[]{:S(2)}) copy-start(bf16[2,4,160,384]{3,2,1,0:T(8,128)(2,1)} %param.10) | copy-start | bytes 2949124
  55.2 6.0 %collective-permute-start.7 = (bf16[1,4,160,384]{3,2,0,1:T(8,128)(2,1)S(1)}, bf16[1,4,160,384]{3,2,0,1:T(8,128)(2,1)}, u32[]{:S(2)}, u32[]{:S(2)}) collective-permute-start(bf16[1,4,160,384]{3,2,0,1:T(8,128)(2,1)S(1)} %fusion.38), channel_id=1, source_target_pairs={} | collective-permute-start | bytes 1474568 | tf_op jit(solution)/shard_map/ppermute | solution.py:10
  56.6 14.5 %collective-permute-start.8 = (bf16[1,4,160,384]{3,2,0,1:T(8,128)(2,1)S(1)}, bf16[1,4,160,384]{3,2,0,1:T(8,128)(2,1)}, u32[]{:S(2)}, u32[]{:S(2)}) collective-permute-start(bf16[1,4,160,384]{3,2,0,1:T(8,128)(2,1)S(1)} %fusion.38), channel_id=1, source_target_pairs={{0,2},{1,3},{4,6},{5,7},{8,10},{9,11},{12,14},{13,15},{16,18},{17,... | collective-permute-start | bytes 1474568 | tf_op jit(solution)/shard_map/ppermute | solution.py:10
  73.1 9.2 %collective-permute-start.9 = (bf16[3,1,160,384]{3,2,1,0:T(8,128)(2,1)}, bf16[3,1,160,384]{3,2,1,0:T(8,128)(2,1)S(1)}, u32[]{:S(2)}, u32[]{:S(2)}) collective-permute-start(bf16[3,1,160,384]{3,2,1,0:T(8,128)(2,1)} %get-tuple-element.7), channel_id=1, source_target_pairs={{0,4},{4,8},{8,12},{1,5},{5,9},{9,13},{2,6},{6,10},{10,14},{3,7},{... | collective-permute-start | bytes 1105928 | tf_op jit(solution)/shard_map/ppermute | solution.py:21
  74.4 11.7 %collective-permute-start.10 = (bf16[3,1,160,384]{3,2,1,0:T(8,128)(2,1)S(1)}, bf16[3,1,160,384]{3,2,1,0:T(8,128)(2,1)S(1)}, u32[]{:S(2)}, u32[]{:S(2)}) collective-permute-start(bf16[3,1,160,384]{3,2,1,0:T(8,128)(2,1)S(1)} %get-tuple-element.8), channel_id=1, source_target_pairs={{4,0},{8,4},{12,8},{5,1},{9,5},{13,9},{6,2},{10,6},{14,10},{7,3},{... | collective-permute-start | bytes 1105928 | tf_op jit(solution)/shard_map/ppermute | solution.py:23
  93.4 2.1 %copy-start.7 = (bf16[3,3,3,384,192]{3,4,2,1,0:T(8,128)(2,1)S(1)}, bf16[3,3,3,384,192]{3,4,2,1,0:T(8,128)(2,1)}, u32[]{:S(2)}) copy-start(bf16[3,3,3,384,192]{3,4,2,1,0:T(8,128)(2,1)} %param.17) | copy-start | bytes 11943940
  93.4 2.1 %copy-start.9 = (pred[8,21]{0,1:T(8,128)(4,1)S(1)}, pred[8,21]{0,1:T(8,128)(4,1)}, u32[]{:S(2)}) copy-start(pred[8,21]{0,1:T(8,128)(4,1)} %constant.101) | copy-start | bytes 508
  95.5 4.2 %copy-start.1 = (bf16[1,4,160,192]{3,2,0,1:T(8,128)(2,1)S(1)}, bf16[1,4,160,192]{3,2,0,1:T(8,128)(2,1)}, u32[]{:S(2)}) copy-start(bf16[1,4,160,192]{3,2,0,1:T(8,128)(2,1)} %constant_dynamic-slice_fusion) | copy-start | bytes 737284
